TPU v7x, 512 devices: a whole 4x8x8 slice. The times are simulated.
512 devices in a mesh: shard: 128 (over y, z, core), tensor: 4 (over x).
Axes of the slice: x: 4, y: 8, z: 8, core: 2. Of those that a mesh axis runs over, the one named last changes fastest.
Arguments:
- grad_query: bfloat16 [128, 1024, 512], P('shard', None, 'tensor'), may hold values from -8 to 8
- error_query: float32 [128, 1024, 512], P('shard', None, 'tensor'), may hold values from -3 to 3
- grad_output: bfloat16 [128, 512, 1024], P('shard', 'tensor'), may hold values from -8 to 8
- error_output: float32 [128, 512, 1024], P('shard', 'tensor'), may hold values from -3 to 3
- start_query: float32 [512, 32], P('tensor'), may hold values from -6 to 6
- start_output: float32 [1024, 32], replicated, may hold values from -6 to 6
- weight_query: float32 [1024, 512], P('shard', 'tensor'), may hold values from -0.1875 to 0.1875
- weight_output: float32 [512, 1024], P('tensor', 'shard'), may hold values from -0.25 to 0.25
- moment_query: float32 [1024, 512], P('shard', 'tensor'), may hold values from -1.2 to 1.2
- moment_output: float32 [512, 1024], P('tensor', 'shard'), may hold values from -1.2 to 1.2
- grad_vector: bfloat16 [128, 3584], P('shard'), may hold values from -12 to 12
- moment_vector: float32 [3584], P('shard'), may hold values from -1.2 to 1.2
- weight_vector: float32 [3584], P('shard'), may hold values from 0.5 to 1.5
Outputs:
- new_error_query: float32 [128, 1024, 512], P('shard', None, 'tensor')
- new_error_output: float32 [128, 512, 1024], P('shard', 'tensor')
- new_moment_query: float32 [1024, 512], P('shard', 'tensor')
- new_moment_output: float32 [512, 1024], P('tensor', 'shard')
- new_weight_query: float32 [1024, 512], P(None, 'tensor')
- new_weight_output: float32 [512, 1024], P('tensor')
- new_moment_vector: float32 [3584], P('shard')
- new_weight_vector: float32 [3584], replicated
All inputs are finite; a program needn't handle non-finite values.
Results may differ from a plain program's by a relative error of at most 0.0003.
Values sent between devices are 32-bit elements; how exact they have to be, the bound alone decides.
No kernel may reach another device: no remote copies, remote signals or barrier semaphores. Data moves between devices by JAX's collectives and lax.ppermute only.
A program may use at most 64 MiB of HBM per device.

v0:
```python
import jax
import jax.numpy as jnp
from jax import lax
from jax.sharding import PartitionSpec as P

ROUNDS = 2
highest = lax.Precision.HIGHEST


def product(left, right):
    return jnp.dot(left, right, precision=highest, preferred_element_type=jnp.float32)


def product_inner(left, right):
    return lax.dot_general(
        left, right, (((0,), (0,)), ((), ())), precision=highest, preferred_element_type=jnp.float32
    )


def solve_rows(gram, factor):
    lower = jnp.linalg.cholesky(gram)
    return jax.scipy.linalg.solve_triangular(lower, factor.T, lower=True).T


def orthonormal(factor):
    return solve_rows(product_inner(factor, factor), factor)


def orthonormal_rows(factor):
    gram = lax.psum(product_inner(factor, factor), "tensor")
    return solve_rows(gram, factor)


def local(
    grad_query,
    error_query,
    grad_output,
    error_output,
    start_query,
    start_output,
    weight_query,
    weight_output,
    moment_query,
    moment_output,
    grad_vector,
    moment_vector,
    weight_vector,
):
    replicas = lax.axis_size("shard")
    shard_index = lax.axis_index("shard")
    total_query = grad_query[0].astype(jnp.float32) + error_query[0]
    total_output = grad_output[0].astype(jnp.float32) + error_output[0]
    factor_query = start_query
    factor_output = start_output
    for turn in range(ROUNDS):
        part_query = product(total_query, factor_query)
        part_output = product(total_output, factor_output)
        sum_query = lax.psum(part_query, ("shard", "tensor"))
        sum_output = lax.psum(part_output, "shard")
        left_query = orthonormal(sum_query)
        left_output = orthonormal_rows(sum_output)
        right_query_part = product_inner(total_query, left_query)
        right_output_part = product_inner(total_output, left_output)
        factor_query = lax.psum(right_query_part, "shard")
        factor_output = lax.psum(right_output_part, ("shard", "tensor"))
    approx_query = product(left_query, factor_query.T) / replicas
    approx_output = product(left_output, factor_output.T) / replicas
    new_error_query = (total_query - approx_query)[None]
    new_error_output = (total_output - approx_output)[None]
    rows_block = moment_query.shape[0]
    block_query = lax.dynamic_slice_in_dim(approx_query, shard_index * rows_block, rows_block, 0)
    cols_block = moment_output.shape[1]
    block_output = lax.dynamic_slice_in_dim(approx_output, shard_index * cols_block, cols_block, 1)
    new_moment_query = 0.9 * moment_query + block_query
    new_moment_output = 0.9 * moment_output + block_output
    stepped_query = weight_query - 0.01 * new_moment_query
    stepped_output = weight_output - 0.01 * new_moment_output
    local_vector = grad_vector[0].astype(jnp.float32)
    vector_block = moment_vector.shape[0]
    vector_whole = lax.psum(local_vector, "shard")
    vector_part = lax.dynamic_slice_in_dim(
        vector_whole, shard_index * vector_block, vector_block, 0
    )
    vector_mean = vector_part / replicas
    new_moment_vector = 0.9 * moment_vector + vector_mean
    stepped_vector = weight_vector - 0.01 * new_moment_vector
    new_weight_query, new_weight_output, new_weight_vector = (
        lax.all_gather(stepped_query, "shard", axis=0, tiled=True),
        lax.all_gather(stepped_output, "shard", axis=1, tiled=True),
        lax.all_gather(stepped_vector, "shard", axis=0, tiled=True),
    )
    return (
        new_error_query,
        new_error_output,
        new_moment_query,
        new_moment_output,
        new_weight_query,
        new_weight_output,
        new_moment_vector,
        new_weight_vector,
    )


def solution(mesh):
    in_specs = (
        P("shard", None, "tensor"),
        P("shard", None, "tensor"),
        P("shard", "tensor", None),
        P("shard", "tensor", None),
        P("tensor", None),
        P(),
        P("shard", "tensor"),
        P("tensor", "shard"),
        P("shard", "tensor"),
        P("tensor", "shard"),
        P("shard", None),
        P("shard"),
        P("shard"),
    )
    out_specs = (
        P("shard", None, "tensor"),
        P("shard", "tensor", None),
        P("shard", "tensor"),
        P("tensor", "shard"),
        P(None, "tensor"),
        P("tensor", None),
        P("shard"),
        P(),
    )
    return jax.shard_map(local, mesh=mesh, in_specs=in_specs, out_specs=out_specs, check_vma=False)
```

profile of v0, /device:TPU:1, one launch (start us, length us, event | category | flops | bytes accessed | tf_op | source)
XLA Modules:
  0.0 2203.4 jit_solution(7634404734054702130)
XLA Ops:
  7.2 1.2 copy.45
  9.1 498.1 %psum.81 = f32[128,32]{0,1:T(8,128)S(1)} all-reduce(f32[128,32]{0,1:T(8,128)S(1)} %fusion.6), channel_id=1, replica_groups=mesh['shard'=128,'tensor'=4] {'shard'}, use_global_device_ids=true, to_apply=%region_6.9 | all-reduce | flops 4096 | bytes 32768 | tf_op jit(solution)/shard_map/psum | solution.py:59
  507.3 13.2 psum.82
  520.6 2.9 cholesky.96
  524.2 0.7 fusion.24
  524.9 2.4 custom-call.12
  527.6 1.3 fusion.4
  528.9 1.3 fusion.15
  530.3 1.3 dynamic-slice
  532.3 265.7 %all-reduce.10.cloned.1.call-done = (f32[1024,32]{0,1:T(8,128)}, f32[1024,32]{0,1:T(8,128)}) async-done(((f32[1024,32]{0,1:T(8,128)}, f32[1024,32]{0,1:T(8,128)}), (f32[1024,32]{0,1:T(8,128)}, f32[1024,32]{0,1:T(8,128)})) %all-reduce.10.cloned.1.call-update) | async-done | bytes 262160 | tf_op jit(solution)/shard_map/psum | solution.py:58
  798.0 1.4 fusion.2
  799.7 2.9 cholesky.74
  804.0 2.4 custom-call.10
  807.2 487.8 %all-reduce.4 = (f32[128,32]{0,1:T(8,128)S(1)}, f32[128,32]{0,1:T(8,128)S(1)}, f32[3584]{0:T(1024)S(1)}) all-reduce(f32[128,32]{0,1:T(8,128)S(1)} %fusion.13, f32[128,32]{0,1:T(8,128)S(1)} %fusion.2, f32[3584]{0:T(1024)S(1)} %convert_reduce_fusion), channel_id=1, replica_groups=mesh['shard'=128,'tensor'=4] {'shard'}, use_global_device_ids=true, to_apply=%region_3.6 | all-reduce | flops 11776 | bytes 94208 | tf_op jit(solution)/shard_map/psum | solution.py:64
  1295.2 12.4 psum.85
  1307.6 2.9 cholesky.107
  1311.9 2.4 custom-call.13
  1314.6 1.3 fusion.11
  1315.9 1.3 fusion
  1318.5 270.5 %all-reduce.8.cloned.1.call-done = (f32[1024,32]{0,1:T(8,128)}, f32[1024,32]{0,1:T(8,128)}) async-done(((f32[1024,32]{0,1:T(8,128)}, f32[1024,32]{0,1:T(8,128)}), (f32[1024,32]{0,1:T(8,128)}, f32[1024,32]{0,1:T(8,128)})) %all-reduce.8.cloned.1.call-update) | async-done | bytes 262160 | tf_op jit(solution)/shard_map/psum | solution.py:58
  1589.0 1.2 fusion.41
  1590.3 2.9 cholesky.85
  1594.6 2.4 custom-call.11
  1597.8 487.8 %all-reduce.3 = (f32[128,32]{0,1:T(8,128)S(1)}, f32[3584]{0:T(1024)}) all-reduce(f32[128,32]{0,1:T(8,128)S(1)} %fusion.9, f32[3584]{0:T(1024)S(1)} %get-tuple-element.48), channel_id=1, replica_groups=mesh['shard'=128,'tensor'=4] {'shard'}, use_global_device_ids=true, to_apply=%region_5.8 | all-reduce | flops 7680 | bytes 61440 | tf_op jit(solution)/shard_map/psum | solution.py:64
  2085.6 1.0 convolution_multiply_fusion.1
  2086.6 0.9 fusion.17
  2087.5 1.0 convolution_multiply_fusion
  2088.6 1.0 copy.52
  2090.2 53.0 %all_gather.10 = f32[128,1024]{0,1:T(8,128)S(1)} all-gather(f32[128,8]{0,1:T(8,128)S(1)} %get-tuple-element.44), channel_id=1, replica_groups=mesh['shard'=128,'tensor'=4] {'shard'}, dimensions={1}, use_global_device_ids=true | all-gather | bytes 528384 | tf_op jit(solution)/shard_map/all_gather | solution.py:89
  2143.3 1.0 copy.53
  2144.9 50.9 %all_gather.9 = f32[1024,128]{1,0:T(8,128)S(1)} all-gather(f32[8,128]{1,0:T(8,128)S(1)} %get-tuple-element.46), channel_id=1, replica_groups=mesh['shard'=128,'tensor'=4] {'shard'}, dimensions={0}, use_global_device_ids=true | all-gather | bytes 528384 | tf_op jit(solution)/shard_map/all_gather | solution.py:88
  2195.8 0.8 copy.63
  (70 shorter events, 10.9 us)
Async XLA Ops:
  7.2 1.5 copy-start
  7.2 1.2 copy-start.5
  7.2 790.8 %all-reduce.10.cloned.1.call-start = ((), (), s32[]{:S(2)}) async-start(), calls=%async_computation.1 | async-start | bytes 524288 | tf_op jit(solution)/shard_map/psum | solution.py:58
  520.6 8.3 copy-start.1
  527.6 1.3 copy-start.2
  527.6 1.3 copy-start.7
  530.3 1058.7 %all-reduce.8.cloned.1.call-start = ((), (), s32[]{:S(2)}) async-start(), calls=%async_computation | async-start | bytes 524288 | tf_op jit(solution)/shard_map/psum | solution.py:58
  530.3 1.9 copy-start.8
  798.0 1.4 copy-start.3
  1317.2 0.7 copy-start.13
  1317.2 0.7 copy-start.14
  1590.2 6.8 copy-start.4
  2086.6 0.9 copy-start.6
  2088.6 1.0 copy-start.9
  2088.6 1.0 copy-start.10
  2143.3 1.0 copy-start.11
  2143.3 1.0 copy-start.12
Sparse Core Ops, SparseCore 0:
  530.4 267.5 all-reduce.9
  1317.3 271.6 all-reduce.7
where the time goes:
time: 2200 us
  blocking collectives  1600 us (73%)
  waiting for transfers between devices  536 us (24%)
  other arithmetic  29.5 us (1%)
    psum x2, blocking collectives, local(): factor_query = lax.psum(right_query_part, 'shard')  976 us
    psum x2, waiting for transfers between devices, local(): sum_query = lax.psum(part_query, ('shard', 'tensor'))  536 us
    psum x1, blocking collectives, local(): sum_output = lax.psum(part_output, 'shard')  498 us
    all_gather x1, blocking collectives, local(): lax.all_gather(stepped_output, 'shard', axis=1, tiled=True)  53 us
    all_gather x1, blocking collectives, local(): lax.all_gather(stepped_query, 'shard', axis=0, tiled=True)  50.9 us
  transfers between devices with their start and end apart: 2, of which 2 were waited for; matrix products, arithmetic and copies ran while one was open for 0% of the time, Pallas kernels for 0%

commit v1 on v0

--- a/solution.py
+++ b/solution.py
@@ -55,7 +55,7 @@
     for turn in range(ROUNDS):
         part_query = product(total_query, factor_query)
         part_output = product(total_output, factor_output)
-        sum_query = lax.psum(part_query, ("shard", "tensor"))
+        sum_query = lax.psum(lax.psum(part_query, "tensor"), "shard")
         sum_output = lax.psum(part_output, "shard")
         left_query = orthonormal(sum_query)
         left_output = orthonormal_rows(sum_output)

time: 2200 us -> 2120 us (0.964)
  blocking collectives: 1600 us -> 1100 us
  waiting for transfers between devices: 536 us -> 944 us
    psum x1 -> x0, blocking collectives: 498 us -> none  [local(): sum_output = lax.psum(part_output, 'shard')]
    psum x2 -> x6, waiting for transfers between devices: 536 us -> 944 us  [the longest x2 476 us: local(): factor_output = lax.psum(right_output_part, ('shard', 'tensor'))]
  transfers between devices with their start and end apart: 2 -> 6, of which waited for: 2 -> 6; matrix products, arithmetic and copies ran while one was open for 0% -> 0% of each run, Pallas kernels for 0% -> 0%
where the time goes in v1:
time: 2120 us
  blocking collectives  1100 us (52%)
  waiting for transfers between devices  944 us (45%)
  other arithmetic  29.5 us (1%)
    psum x2, blocking collectives, local(): factor_query = lax.psum(right_query_part, 'shard')  973 us
    psum x2, waiting for transfers between devices, local(): factor_output = lax.psum(right_output_part, ('shard', 'tensor'))  476 us
    psum x4, waiting for transfers between devices, local(): sum_query = lax.psum(lax.psum(part_query, 'tensor'), 'shard')  468 us
    all_gather x1, blocking collectives, local(): lax.all_gather(stepped_query, 'shard', axis=0, tiled=True)  55.5 us
    all_gather x1, blocking collectives, local(): lax.all_gather(stepped_output, 'shard', axis=1, tiled=True)  49 us
  transfers between devices with their start and end apart: 6, of which 6 were waited for; matrix products, arithmetic and copies ran while one was open for 0% of the time, Pallas kernels for 0%

profile of v1, /device:TPU:1, one launch (start us, length us, event | category | flops | bytes accessed | tf_op | source)
XLA Modules:
  0.0 2115.6 jit_solution(723833185253901209)
XLA Ops:
  7.2 2.5 fusion.15
  11.0 1.3 dynamic-slice
  13.4 52.8 %all-reduce.10.cloned.1.call-done = f32[1024,32]{0,1:T(8,128)} async-done(((f32[1024,32]{0,1:T(8,128)}), f32[1024,32]{0,1:T(8,128)}) %all-reduce.10.cloned.1.call-update) | async-done | bytes 131088 | tf_op jit(solution)/shard_map/psum | solution.py:58
  66.3 188.7 %all-reduce.12.cloned.1.call-done = f32[1024,32]{0,1:T(8,128)} async-done(((f32[1024,32]{0,1:T(8,128)}), f32[1024,32]{0,1:T(8,128)}) %all-reduce.12.cloned.1.call-update) | async-done | bytes 131088 | tf_op jit(solution)/shard_map/psum | solution.py:58
  255.0 1.2 fusion.40
  256.4 2.9 cholesky.74
  260.6 2.4 custom-call.10
  263.0 1.2 fusion.20
  264.8 486.4 %all-reduce.2 = (f32[128,32]{0,1:T(8,128)S(1)}, f32[128,32]{0,1:T(8,128)S(1)}, f32[3584]{0:T(1024)S(1)}) all-reduce(f32[128,32]{0,1:T(8,128)S(1)} %fusion.13, f32[128,32]{0,1:T(8,128)S(1)} %fusion.6, f32[3584]{0:T(1024)S(1)} %convert_reduce_fusion), channel_id=1, replica_groups=mesh['shard'=128,'tensor'=4] {'shard'}, use_global_device_ids=true, to_apply=%region_4.7 | all-reduce | flops 11776 | bytes 94208 | tf_op jit(solution)/shard_map/psum | solution.py:64
  751.3 13.2 psum.98
  764.6 2.9 cholesky.96
  768.8 2.4 custom-call.12
  771.5 1.3 fusion.11
  772.9 1.3 fusion.4
  775.6 48.7 %all-reduce.14.cloned.1.call-done = f32[1024,32]{0,1:T(8,128)} async-done(((f32[1024,32]{0,1:T(8,128)}), f32[1024,32]{0,1:T(8,128)}) %all-reduce.14.cloned.1.call-update) | async-done | bytes 131088 | tf_op jit(solution)/shard_map/psum | solution.py:58
  824.3 269.6 %all-reduce.18.cloned.1.call-done = f32[1024,32]{0,1:T(8,128)} async-done(((f32[1024,32]{0,1:T(8,128)}), f32[1024,32]{0,1:T(8,128)}) %all-reduce.18.cloned.1.call-update) | async-done | bytes 131088 | tf_op jit(solution)/shard_map/psum | solution.py:65
  1094.0 1.3 fusion.2
  1095.3 178.2 %all-reduce.16.cloned.1.call-done = f32[1024,32]{0,1:T(8,128)} async-done(((f32[1024,32]{0,1:T(8,128)}), f32[1024,32]{0,1:T(8,128)}) %all-reduce.16.cloned.1.call-update) | async-done | bytes 131088 | tf_op jit(solution)/shard_map/psum | solution.py:58
  1273.5 1.2 fusion.41
  1274.8 2.9 cholesky.85
  1279.1 2.4 custom-call.11
  1282.3 486.4 %all-reduce.1 = (f32[128,32]{0,1:T(8,128)S(1)}, f32[128,32]{0,1:T(8,128)S(1)}, f32[3584]{0:T(1024)}) all-reduce(f32[128,32]{0,1:T(8,128)S(1)} %fusion.9, f32[128,32]{0,1:T(8,128)S(1)} %fusion.2, f32[3584]{0:T(1024)S(1)} %get-tuple-element.45), channel_id=1, replica_groups=mesh['shard'=128,'tensor'=4] {'shard'}, use_global_device_ids=true, to_apply=%region_7.10 | all-reduce | flops 11776 | bytes 94208 | tf_op jit(solution)/shard_map/psum | solution.py:64
  1768.8 13.2 psum.101
  1782.1 2.9 cholesky.107
  1786.4 2.4 custom-call.13
  1789.0 1.3 fusion
  1790.4 1.0 convolution_multiply_fusion.1
  1792.9 55.5 %all_gather.9 = f32[1024,128]{1,0:T(8,128)S(1)} all-gather(f32[8,128]{1,0:T(8,128)S(1)} %get-tuple-element.43), channel_id=1, replica_groups=mesh['shard'=128,'tensor'=4] {'shard'}, dimensions={0}, use_global_device_ids=true | all-gather | bytes 528384 | tf_op jit(solution)/shard_map/all_gather | solution.py:88
  1848.4 205.9 %all-reduce.20.cloned.1.call-done = f32[1024,32]{0,1:T(8,128)} async-done(((f32[1024,32]{0,1:T(8,128)}), f32[1024,32]{0,1:T(8,128)}) %all-reduce.20.cloned.1.call-update) | async-done | bytes 131088 | tf_op jit(solution)/shard_map/psum | solution.py:65
  2054.3 1.9 convolution_multiply_fusion
  2056.3 1.0 copy.52
  2057.9 49.0 %all_gather.10 = f32[128,1024]{0,1:T(8,128)S(1)} all-gather(f32[128,8]{0,1:T(8,128)S(1)} %get-tuple-element.41), channel_id=1, replica_groups=mesh['shard'=128,'tensor'=4] {'shard'}, dimensions={1}, use_global_device_ids=true | all-gather | bytes 528384 | tf_op jit(solution)/shard_map/all_gather | solution.py:89
  (77 shorter events, 14.8 us)
Async XLA Ops:
  7.2 5.7 copy-start
  7.2 59.0 %all-reduce.10.cloned.1.call-start = ((), (), s32[]{:S(2)}) async-start(), calls=%async_computation | async-start | bytes 262144 | tf_op jit(solution)/shard_map/psum | solution.py:58
  7.2 2.6 copy-start.5
  9.7 1.0 copy-start.4
  9.7 245.3 %all-reduce.12.cloned.1.call-start = ((), (), s32[]{:S(2)}) async-start(), calls=%async_computation.1 | async-start | bytes 262144 | tf_op jit(solution)/shard_map/psum | solution.py:58
  12.9 53.4 %copy-start.6 = (bf16[1,3584]{1,0:T(2,128)(2,1)S(1)}, bf16[1,3584]{1,0:T(2,128)(2,1)}, u32[]{:S(2)}) copy-start(bf16[1,3584]{1,0:T(2,128)(2,1)} %param.28) | copy-start | bytes 21508
  13.3 251.0 %copy-start.1 = (f32[1,1024,128]{2,1,0:T(8,128)S(1)}, f32[1,1024,128]{2,1,0:T(8,128)}, u32[]{:S(2)}) copy-start(f32[1,1024,128]{2,1,0:T(8,128)} %param.19) | copy-start | bytes 1572868
  66.2 758.0 %all-reduce.14.cloned.1.call-start = ((), (), s32[]{:S(2)}) async-start(), calls=%async_computation.2 | async-start | bytes 262144 | tf_op jit(solution)/shard_map/psum | solution.py:58
  256.3 8.0 copy-start.2
  772.8 321.1 %all-reduce.18.cloned.1.call-start = ((), (), s32[]{:S(2)}) async-start(), calls=%async_computation.4 | async-start | bytes 262144 | tf_op jit(solution)/shard_map/psum | solution.py:65
  774.2 499.2 %all-reduce.16.cloned.1.call-start = ((), (), s32[]{:S(2)}) async-start(), calls=%async_computation.3 | async-start | bytes 262144 | tf_op jit(solution)/shard_map/psum | solution.py:58
  774.3 0.7 copy-start.11
  774.3 0.7 copy-start.12
  824.3 1230.0 %all-reduce.20.cloned.1.call-start = ((), (), s32[]{:S(2)}) async-start(), calls=%async_computation.5 | async-start | bytes 262144 | tf_op jit(solution)/shard_map/psum | solution.py:65
  1274.7 6.8 copy-start.3
  1791.4 0.9 copy-start.7
  1791.4 0.9 copy-start.8
  2056.3 1.0 copy-start.9
  2056.3 1.0 copy-start.10
Sparse Core Ops, SparseCore 0:
  10.9 55.2 all-reduce.9
  69.8 185.1 all-reduce.11
  773.0 51.2 all-reduce.13
  829.7 264.2 all-reduce.17
  1097.4 176.0 all-reduce.15
  1790.5 263.7 all-reduce.19
